TPU v7x, 32 devices: a whole 2x2x4 slice. The times are simulated.
32 devices in a mesh: groups: 2 (over x), orient: 8 (over z, y), tile: 2 (over core).
Axes of the slice: x: 2, y: 2, z: 4, core: 2. Of those that a mesh axis runs over, the one named last changes fastest.
Arguments:
- spectra: float32 [16, 2, 256, 256], P(('groups', 'orient'), None, 'tile'), parts along dimension 0, may hold values from -6 to 6
- templates: float32 [8, 2, 256, 256], P('orient', None, 'tile'), may hold values from -1600 to 1600, as said below
- weights: float32 [512, 256], P('groups'), parts along dimension 0, may hold values from 0.1 to 1
Outputs:
- peak: float32 [16, 256, 256], P(('groups', 'orient'), 'tile'), parts along dimension 0
- mean_map: float32 [16, 256, 256], P(('groups', 'orient'), 'tile'), parts along dimension 0
- mean_square: float32 [16, 256, 256], P(('groups', 'orient'), 'tile'), parts along dimension 0
There are 2 independent parts, one for each index of `groups`. A program takes and returns all parts, laid end to end along the dimension named above; an argument that names none is the same for every part. Nothing has to cross between parts.
Inputs may be any that keep to these rules, and one draw needn't show every extreme that they name: `templates`: finite real values.
All inputs are finite; a program needn't handle non-finite values.
Results may differ from a plain program's by a relative error of at most 0.00029.
Values sent between devices are 32-bit elements; how exact they have to be, the bound alone decides.
A program may use at most 64 MiB of HBM per device.

v0:
```python
import math

import jax
import jax.numpy as jnp
from jax import lax
from jax.sharding import PartitionSpec as P


def shifted(x, axis, by):
    peers = lax.axis_size(axis)
    return lax.ppermute(x, axis, [(i, (i + by) % peers) for i in range(peers)])


def twiddle(rows, cols, side):
    phase = rows[:, None] * cols[None, :] % side
    angle = phase.astype(jnp.float32) * (2.0 * math.pi / side)
    return (jnp.cos(angle), jnp.sin(angle))


def shards(spectra, templates, weights):
    side = spectra.shape[3]
    half = spectra.shape[2]
    n_orient = lax.axis_size("orient")
    out_rows = lax.axis_index("tile") * half + lax.iota(jnp.int32, half)
    freq = lax.iota(jnp.int32, side)
    row_cos, row_sin = twiddle(out_rows, freq, side)
    col_cos, col_sin = twiddle(freq, freq, side)
    row_table = jnp.concatenate([row_cos, row_sin], 0)
    highest = lax.Precision.HIGHEST
    whole_templates = lax.all_gather(templates, "tile", axis=2, tiled=True)
    power = jnp.mean(whole_templates * whole_templates, axis=(1, 2, 3), keepdims=True)
    scaling = jnp.sqrt(power + 1e-06)

    def correlate(full, template):
        real_part = (full[:, 0] * template[0] + full[:, 1] * template[1]) * weights
        imag_part = (full[:, 1] * template[0] - full[:, 0] * template[1]) * weights
        stack_real = jnp.einsum("yk,nkx->nyx", row_table, real_part, precision=highest)
        stack_imag = jnp.einsum("yk,nkx->nyx", row_table, imag_part, precision=highest)
        along_real = stack_real[:, :half] - stack_imag[:, half:]
        along_imag = stack_imag[:, :half] + stack_real[:, half:]
        maps = jnp.einsum("nyk,kx->nyx", along_real, col_cos, precision=highest)
        maps = maps - jnp.einsum("nyk,kx->nyx", along_imag, col_sin, precision=highest)
        return maps / side

    def absorb(stats, full, pieces):

        def one_orientation(carry, template):
            maps = correlate(full, template)
            best, total, squares = carry
            return ((jnp.maximum(best, maps), total + maps, squares + maps * maps), None)

        result, _ = lax.scan(one_orientation, stats, pieces)
        return result

    stat_shape = (spectra.shape[0], half, side)
    initial = (
        jnp.full(stat_shape, -jnp.inf, jnp.float32),
        jnp.zeros(stat_shape, jnp.float32),
        jnp.zeros(stat_shape, jnp.float32),
    )
    normed = whole_templates / scaling

    def visit(step, carry):
        held, best, total, squares = carry
        full = lax.all_gather(held, "tile", axis=2, tiled=True)
        best, total, squares = absorb((best, total, squares), full, normed)
        return shifted((held, best, total, squares), "orient", 1)

    _, best, total, squares = lax.fori_loop(0, n_orient, visit, (spectra,) + initial)
    count = n_orient * templates.shape[0]
    return (best, total / count, squares / count)


def solution(mesh):
    in_specs = (
        P(("groups", "orient"), None, "tile", None),
        P("orient", None, "tile", None),
        P("groups", None),
    )
    out_specs = (
        P(("groups", "orient"), "tile", None),
        P(("groups", "orient"), "tile", None),
        P(("groups", "orient"), "tile", None),
    )
    return jax.shard_map(shards, mesh=mesh, in_specs=in_specs, out_specs=out_specs, check_vma=False)
```

profile of v0, /device:TPU:0, one launch (start us, length us, event | category | flops | bytes accessed | tf_op | source)
XLA Modules:
  0.0 173.7 jit_solution(17262018775637251267)
XLA Ops:
  2.2 2.2 %all_gather.6 = f32[1,2,256,256]{3,2,1,0:T(8,128)S(1)} all-gather(f32[1,2,128,256]{3,2,1,0:T(8,128)S(1)} %copy-done.2), channel_id=1, replica_groups=mesh['groups'=2,'orient'=8,'tile'=2] {'tile'}, dimensions={2}, use_global_device_ids=true | all-gather | bytes 786432 | tf_op jit(solution)/shard_map/all_gather | solution.py:30
  6.9 165.4 %while.16 = (s32[]{:T(128)}, f32[1,2,128,256]{3,2,1,0:T(8,128)S(1)}, f32[1,128,256]{2,1,0:T(8,128)S(1)}, f32[1,128,256]{2,1,0:T(8,128)S(1)}, f32[1,128,256]{2,1,...) while((s32[]{:T(128)}, ...), condition=%wide.region_2.3_spmd.clone, body=%wide.region_1.2_spmd.clone.sunk | while | flops 606601216 | bytes 9175293 | solution.py:69
  6.9 2.9 %collective-permute-start = (f32[1,2,128,256]{3,2,1,0:T(8,128)S(1)}, f32[1,2,128,256]{3,2,1,0:T(8,128)S(1)}, u32[]{:S(2)}, u32[]{:S(2)}) collective-permute-start(f32[1,2,128,256]{3,2,1,0:T(8,128)S(1)} %copy.12), channel_id=1, source_target_pairs={{0,2},{2,4},{4,6},{6,8},{8,10},{10,12},{12,14},{14,0},{1,3},{3,5},... | collective-permute-start | bytes 786440 | tf_op jit(solution)/shard_map/while/body/eval_jaxpr/ppermute | solution.py:11
  20.6 4.5 %collective-permute-done.1 = f32[1,128,256]{2,1,0:T(8,128)S(1)} collective-permute-done((f32[1,128,256]{2,1,0:T(8,128)S(1)}, f32[1,128,256]{2,1,0:T(8,128)S(1)}, u32[]{:S(2)}, u32[]{:S(2)}) %collective-permute-start.1) | collective-permute-done | bytes 131104 | tf_op jit(solution)/shard_map/while/body/eval_jaxpr/ppermute | solution.py:11
  25.0 2.8 %collective-permute-done.2 = f32[1,128,256]{2,1,0:T(8,128)S(1)} collective-permute-done((f32[1,128,256]{2,1,0:T(8,128)S(1)}, f32[1,128,256]{2,1,0:T(8,128)S(1)}, u32[]{:S(2)}, u32[]{:S(2)}) %collective-permute-start.2) | collective-permute-done | bytes 131104 | tf_op jit(solution)/shard_map/while/body/eval_jaxpr/ppermute | solution.py:11
  30.0 2.2 %all_gather.9 = f32[1,2,256,256]{3,2,1,0:T(8,128)S(1)} all-gather(f32[1,2,128,256]{3,2,1,0:T(8,128)S(1)} %copy.12), channel_id=1, replica_groups=mesh['groups'=2,'orient'=8,'tile'=2] {'tile'}, dimensions={2}, use_global_device_ids=true | all-gather | bytes 786432 | tf_op jit(solution)/shard_map/while/body/eval_jaxpr/all_gather | solution.py:65
  37.9 2.4 %collective-permute-start.3 = (f32[1,128,256]{2,1,0:T(8,128)S(1)}, f32[1,128,256]{2,1,0:T(8,128)S(1)}, u32[]{:S(2)}, u32[]{:S(2)}) collective-permute-start(f32[1,128,256]{2,1,0:T(8,128)S(1)} %get-tuple-element.186), channel_id=1, source_target_pairs={{0,2},{2,4},{4,6},{6,8},{8,10},{10,12},{12,14},{14,0},{1,3},{3,5},... | collective-permute-start | bytes 393224 | tf_op jit(solution)/shard_map/while/body/eval_jaxpr/ppermute | solution.py:11
  40.4 4.7 %collective-permute-done.1 = f32[1,128,256]{2,1,0:T(8,128)S(1)} collective-permute-done((f32[1,128,256]{2,1,0:T(8,128)S(1)}, f32[1,128,256]{2,1,0:T(8,128)S(1)}, u32[]{:S(2)}, u32[]{:S(2)}) %collective-permute-start.1) | collective-permute-done | bytes 131104 | tf_op jit(solution)/shard_map/while/body/eval_jaxpr/ppermute | solution.py:11
  45.1 2.8 %collective-permute-done.2 = f32[1,128,256]{2,1,0:T(8,128)S(1)} collective-permute-done((f32[1,128,256]{2,1,0:T(8,128)S(1)}, f32[1,128,256]{2,1,0:T(8,128)S(1)}, u32[]{:S(2)}, u32[]{:S(2)}) %collective-permute-start.2) | collective-permute-done | bytes 131104 | tf_op jit(solution)/shard_map/while/body/eval_jaxpr/ppermute | solution.py:11
  47.9 2.3 %collective-permute-done.3 = f32[1,128,256]{2,1,0:T(8,128)S(1)} collective-permute-done((f32[1,128,256]{2,1,0:T(8,128)S(1)}, f32[1,128,256]{2,1,0:T(8,128)S(1)}, u32[]{:S(2)}, u32[]{:S(2)}) %collective-permute-start.3) | collective-permute-done | bytes 131104 | tf_op jit(solution)/shard_map/while/body/eval_jaxpr/ppermute | solution.py:11
  50.3 2.2 %all_gather.9 = f32[1,2,256,256]{3,2,1,0:T(8,128)S(1)} all-gather(f32[1,2,128,256]{3,2,1,0:T(8,128)S(1)} %copy.12), channel_id=1, replica_groups=mesh['groups'=2,'orient'=8,'tile'=2] {'tile'}, dimensions={2}, use_global_device_ids=true | all-gather | bytes 786432 | tf_op jit(solution)/shard_map/while/body/eval_jaxpr/all_gather | solution.py:65
  59.3 6.2 %collective-permute-done.1 = f32[1,128,256]{2,1,0:T(8,128)S(1)} collective-permute-done((f32[1,128,256]{2,1,0:T(8,128)S(1)}, f32[1,128,256]{2,1,0:T(8,128)S(1)}, u32[]{:S(2)}, u32[]{:S(2)}) %collective-permute-start.1) | collective-permute-done | bytes 131104 | tf_op jit(solution)/shard_map/while/body/eval_jaxpr/ppermute | solution.py:11
  65.5 2.8 %collective-permute-done.2 = f32[1,128,256]{2,1,0:T(8,128)S(1)} collective-permute-done((f32[1,128,256]{2,1,0:T(8,128)S(1)}, f32[1,128,256]{2,1,0:T(8,128)S(1)}, u32[]{:S(2)}, u32[]{:S(2)}) %collective-permute-start.2) | collective-permute-done | bytes 131104 | tf_op jit(solution)/shard_map/while/body/eval_jaxpr/ppermute | solution.py:11
  68.3 2.3 %collective-permute-done.3 = f32[1,128,256]{2,1,0:T(8,128)S(1)} collective-permute-done((f32[1,128,256]{2,1,0:T(8,128)S(1)}, f32[1,128,256]{2,1,0:T(8,128)S(1)}, u32[]{:S(2)}, u32[]{:S(2)}) %collective-permute-start.3) | collective-permute-done | bytes 131104 | tf_op jit(solution)/shard_map/while/body/eval_jaxpr/ppermute | solution.py:11
  70.7 2.2 %all_gather.9 = f32[1,2,256,256]{3,2,1,0:T(8,128)S(1)} all-gather(f32[1,2,128,256]{3,2,1,0:T(8,128)S(1)} %copy.12), channel_id=1, replica_groups=mesh['groups'=2,'orient'=8,'tile'=2] {'tile'}, dimensions={2}, use_global_device_ids=true | all-gather | bytes 786432 | tf_op jit(solution)/shard_map/while/body/eval_jaxpr/all_gather | solution.py:65
  79.0 6.8 %collective-permute-done.1 = f32[1,128,256]{2,1,0:T(8,128)S(1)} collective-permute-done((f32[1,128,256]{2,1,0:T(8,128)S(1)}, f32[1,128,256]{2,1,0:T(8,128)S(1)}, u32[]{:S(2)}, u32[]{:S(2)}) %collective-permute-start.1) | collective-permute-done | bytes 131104 | tf_op jit(solution)/shard_map/while/body/eval_jaxpr/ppermute | solution.py:11
  85.8 2.8 %collective-permute-done.2 = f32[1,128,256]{2,1,0:T(8,128)S(1)} collective-permute-done((f32[1,128,256]{2,1,0:T(8,128)S(1)}, f32[1,128,256]{2,1,0:T(8,128)S(1)}, u32[]{:S(2)}, u32[]{:S(2)}) %collective-permute-start.2) | collective-permute-done | bytes 131104 | tf_op jit(solution)/shard_map/while/body/eval_jaxpr/ppermute | solution.py:11
  88.6 2.3 %collective-permute-done.3 = f32[1,128,256]{2,1,0:T(8,128)S(1)} collective-permute-done((f32[1,128,256]{2,1,0:T(8,128)S(1)}, f32[1,128,256]{2,1,0:T(8,128)S(1)}, u32[]{:S(2)}, u32[]{:S(2)}) %collective-permute-start.3) | collective-permute-done | bytes 131104 | tf_op jit(solution)/shard_map/while/body/eval_jaxpr/ppermute | solution.py:11
  91.0 2.2 %all_gather.9 = f32[1,2,256,256]{3,2,1,0:T(8,128)S(1)} all-gather(f32[1,2,128,256]{3,2,1,0:T(8,128)S(1)} %copy.12), channel_id=1, replica_groups=mesh['groups'=2,'orient'=8,'tile'=2] {'tile'}, dimensions={2}, use_global_device_ids=true | all-gather | bytes 786432 | tf_op jit(solution)/shard_map/while/body/eval_jaxpr/all_gather | solution.py:65
  97.7 8.5 %collective-permute-done.1 = f32[1,128,256]{2,1,0:T(8,128)S(1)} collective-permute-done((f32[1,128,256]{2,1,0:T(8,128)S(1)}, f32[1,128,256]{2,1,0:T(8,128)S(1)}, u32[]{:S(2)}, u32[]{:S(2)}) %collective-permute-start.1) | collective-permute-done | bytes 131104 | tf_op jit(solution)/shard_map/while/body/eval_jaxpr/ppermute | solution.py:11
  106.2 2.8 %collective-permute-done.2 = f32[1,128,256]{2,1,0:T(8,128)S(1)} collective-permute-done((f32[1,128,256]{2,1,0:T(8,128)S(1)}, f32[1,128,256]{2,1,0:T(8,128)S(1)}, u32[]{:S(2)}, u32[]{:S(2)}) %collective-permute-start.2) | collective-permute-done | bytes 131104 | tf_op jit(solution)/shard_map/while/body/eval_jaxpr/ppermute | solution.py:11
  109.0 2.3 %collective-permute-done.3 = f32[1,128,256]{2,1,0:T(8,128)S(1)} collective-permute-done((f32[1,128,256]{2,1,0:T(8,128)S(1)}, f32[1,128,256]{2,1,0:T(8,128)S(1)}, u32[]{:S(2)}, u32[]{:S(2)}) %collective-permute-start.3) | collective-permute-done | bytes 131104 | tf_op jit(solution)/shard_map/while/body/eval_jaxpr/ppermute | solution.py:11
  111.4 2.2 %all_gather.9 = f32[1,2,256,256]{3,2,1,0:T(8,128)S(1)} all-gather(f32[1,2,128,256]{3,2,1,0:T(8,128)S(1)} %copy.12), channel_id=1, replica_groups=mesh['groups'=2,'orient'=8,'tile'=2] {'tile'}, dimensions={2}, use_global_device_ids=true | all-gather | bytes 786432 | tf_op jit(solution)/shard_map/while/body/eval_jaxpr/all_gather | solution.py:65
  118.2 8.4 %collective-permute-done.1 = f32[1,128,256]{2,1,0:T(8,128)S(1)} collective-permute-done((f32[1,128,256]{2,1,0:T(8,128)S(1)}, f32[1,128,256]{2,1,0:T(8,128)S(1)}, u32[]{:S(2)}, u32[]{:S(2)}) %collective-permute-start.1) | collective-permute-done | bytes 131104 | tf_op jit(solution)/shard_map/while/body/eval_jaxpr/ppermute | solution.py:11
  126.5 2.8 %collective-permute-done.2 = f32[1,128,256]{2,1,0:T(8,128)S(1)} collective-permute-done((f32[1,128,256]{2,1,0:T(8,128)S(1)}, f32[1,128,256]{2,1,0:T(8,128)S(1)}, u32[]{:S(2)}, u32[]{:S(2)}) %collective-permute-start.2) | collective-permute-done | bytes 131104 | tf_op jit(solution)/shard_map/while/body/eval_jaxpr/ppermute | solution.py:11
  129.3 2.3 %collective-permute-done.3 = f32[1,128,256]{2,1,0:T(8,128)S(1)} collective-permute-done((f32[1,128,256]{2,1,0:T(8,128)S(1)}, f32[1,128,256]{2,1,0:T(8,128)S(1)}, u32[]{:S(2)}, u32[]{:S(2)}) %collective-permute-start.3) | collective-permute-done | bytes 131104 | tf_op jit(solution)/shard_map/while/body/eval_jaxpr/ppermute | solution.py:11
  138.5 8.4 %collective-permute-done.1 = f32[1,128,256]{2,1,0:T(8,128)S(1)} collective-permute-done((f32[1,128,256]{2,1,0:T(8,128)S(1)}, f32[1,128,256]{2,1,0:T(8,128)S(1)}, u32[]{:S(2)}, u32[]{:S(2)}) %collective-permute-start.1) | collective-permute-done | bytes 131104 | tf_op jit(solution)/shard_map/while/body/eval_jaxpr/ppermute | solution.py:11
  146.9 2.8 %collective-permute-done.2 = f32[1,128,256]{2,1,0:T(8,128)S(1)} collective-permute-done((f32[1,128,256]{2,1,0:T(8,128)S(1)}, f32[1,128,256]{2,1,0:T(8,128)S(1)}, u32[]{:S(2)}, u32[]{:S(2)}) %collective-permute-start.2) | collective-permute-done | bytes 131104 | tf_op jit(solution)/shard_map/while/body/eval_jaxpr/ppermute | solution.py:11
  149.7 2.3 %collective-permute-done.3 = f32[1,128,256]{2,1,0:T(8,128)S(1)} collective-permute-done((f32[1,128,256]{2,1,0:T(8,128)S(1)}, f32[1,128,256]{2,1,0:T(8,128)S(1)}, u32[]{:S(2)}, u32[]{:S(2)}) %collective-permute-start.3) | collective-permute-done | bytes 131104 | tf_op jit(solution)/shard_map/while/body/eval_jaxpr/ppermute | solution.py:11
  158.9 8.4 %collective-permute-done.1 = f32[1,128,256]{2,1,0:T(8,128)S(1)} collective-permute-done((f32[1,128,256]{2,1,0:T(8,128)S(1)}, f32[1,128,256]{2,1,0:T(8,128)S(1)}, u32[]{:S(2)}, u32[]{:S(2)}) %collective-permute-start.1) | collective-permute-done | bytes 131104 | tf_op jit(solution)/shard_map/while/body/eval_jaxpr/ppermute | solution.py:11
  167.2 2.8 %collective-permute-done.2 = f32[1,128,256]{2,1,0:T(8,128)S(1)} collective-permute-done((f32[1,128,256]{2,1,0:T(8,128)S(1)}, f32[1,128,256]{2,1,0:T(8,128)S(1)}, u32[]{:S(2)}, u32[]{:S(2)}) %collective-permute-start.2) | collective-permute-done | bytes 131104 | tf_op jit(solution)/shard_map/while/body/eval_jaxpr/ppermute | solution.py:11
  170.0 2.3 %collective-permute-done.3 = f32[1,128,256]{2,1,0:T(8,128)S(1)} collective-permute-done((f32[1,128,256]{2,1,0:T(8,128)S(1)}, f32[1,128,256]{2,1,0:T(8,128)S(1)}, u32[]{:S(2)}, u32[]{:S(2)}) %collective-permute-start.3) | collective-permute-done | bytes 131104 | tf_op jit(solution)/shard_map/while/body/eval_jaxpr/ppermute | solution.py:11
  (98 shorter events, 59.0 us)
Async XLA Ops:
  6.9 22.9 %collective-permute-start = (f32[1,2,128,256]{3,2,1,0:T(8,128)S(1)}, f32[1,2,128,256]{3,2,1,0:T(8,128)S(1)}, u32[]{:S(2)}, u32[]{:S(2)}) collective-permute-start(f32[1,2,128,256]{3,2,1,0:T(8,128)S(1)} %copy.12), channel_id=1, source_target_pairs={{0,2},{2,4},{4,6},{6,8},{8,10},{10,12},{12,14},{14,0},{1,3},{3,5},... | collective-permute-start | bytes 786440 | tf_op jit(solution)/shard_map/while/body/eval_jaxpr/ppermute | solution.py:11
  16.0 9.1 %collective-permute-start.1 = (f32[1,128,256]{2,1,0:T(8,128)S(1)}, f32[1,128,256]{2,1,0:T(8,128)S(1)}, u32[]{:S(2)}, u32[]{:S(2)}) collective-permute-start(f32[1,128,256]{2,1,0:T(8,128)S(1)} %get-tuple-element.184), channel_id=1, source_target_pairs={{0,2},{2,4},{4,6},{6,8},{8,10},{10,12},{12,14},{14,0},{1,3},{3,5},... | collective-permute-start | bytes 393224 | tf_op jit(solution)/shard_map/while/body/eval_jaxpr/ppermute | solution.py:11
  17.5 10.3 %collective-permute-start.2 = (f32[1,128,256]{2,1,0:T(8,128)S(1)}, f32[1,128,256]{2,1,0:T(8,128)S(1)}, u32[]{:S(2)}, u32[]{:S(2)}) collective-permute-start(f32[1,128,256]{2,1,0:T(8,128)S(1)} %get-tuple-element.185), channel_id=1, source_target_pairs={{0,2},{2,4},{4,6},{6,8},{8,10},{10,12},{12,14},{14,0},{1,3},{3,5},... | collective-permute-start | bytes 393224 | tf_op jit(solution)/shard_map/while/body/eval_jaxpr/ppermute | solution.py:11
  19.1 10.8 %collective-permute-start.3 = (f32[1,128,256]{2,1,0:T(8,128)S(1)}, f32[1,128,256]{2,1,0:T(8,128)S(1)}, u32[]{:S(2)}, u32[]{:S(2)}) collective-permute-start(f32[1,128,256]{2,1,0:T(8,128)S(1)} %get-tuple-element.186), channel_id=1, source_target_pairs={{0,2},{2,4},{4,6},{6,8},{8,10},{10,12},{12,14},{14,0},{1,3},{3,5},... | collective-permute-start | bytes 393224 | tf_op jit(solution)/shard_map/while/body/eval_jaxpr/ppermute | solution.py:11
  29.9 20.3 %collective-permute-start = (f32[1,2,128,256]{3,2,1,0:T(8,128)S(1)}, f32[1,2,128,256]{3,2,1,0:T(8,128)S(1)}, u32[]{:S(2)}, u32[]{:S(2)}) collective-permute-start(f32[1,2,128,256]{3,2,1,0:T(8,128)S(1)} %copy.12), channel_id=1, source_target_pairs={{0,2},{2,4},{4,6},{6,8},{8,10},{10,12},{12,14},{14,0},{1,3},{3,5},... | collective-permute-start | bytes 786440 | tf_op jit(solution)/shard_map/while/body/eval_jaxpr/ppermute | solution.py:11
  36.1 9.1 %collective-permute-start.1 = (f32[1,128,256]{2,1,0:T(8,128)S(1)}, f32[1,128,256]{2,1,0:T(8,128)S(1)}, u32[]{:S(2)}, u32[]{:S(2)}) collective-permute-start(f32[1,128,256]{2,1,0:T(8,128)S(1)} %get-tuple-element.184), channel_id=1, source_target_pairs={{0,2},{2,4},{4,6},{6,8},{8,10},{10,12},{12,14},{14,0},{1,3},{3,5},... | collective-permute-start | bytes 393224 | tf_op jit(solution)/shard_map/while/body/eval_jaxpr/ppermute | solution.py:11
  37.3 10.6 %collective-permute-start.2 = (f32[1,128,256]{2,1,0:T(8,128)S(1)}, f32[1,128,256]{2,1,0:T(8,128)S(1)}, u32[]{:S(2)}, u32[]{:S(2)}) collective-permute-start(f32[1,128,256]{2,1,0:T(8,128)S(1)} %get-tuple-element.185), channel_id=1, source_target_pairs={{0,2},{2,4},{4,6},{6,8},{8,10},{10,12},{12,14},{14,0},{1,3},{3,5},... | collective-permute-start | bytes 393224 | tf_op jit(solution)/shard_map/while/body/eval_jaxpr/ppermute | solution.py:11
  37.9 12.3 %collective-permute-start.3 = (f32[1,128,256]{2,1,0:T(8,128)S(1)}, f32[1,128,256]{2,1,0:T(8,128)S(1)}, u32[]{:S(2)}, u32[]{:S(2)}) collective-permute-start(f32[1,128,256]{2,1,0:T(8,128)S(1)} %get-tuple-element.186), channel_id=1, source_target_pairs={{0,2},{2,4},{4,6},{6,8},{8,10},{10,12},{12,14},{14,0},{1,3},{3,5},... | collective-permute-start | bytes 393224 | tf_op jit(solution)/shard_map/while/body/eval_jaxpr/ppermute | solution.py:11
  50.2 20.3 %collective-permute-start = (f32[1,2,128,256]{3,2,1,0:T(8,128)S(1)}, f32[1,2,128,256]{3,2,1,0:T(8,128)S(1)}, u32[]{:S(2)}, u32[]{:S(2)}) collective-permute-start(f32[1,2,128,256]{3,2,1,0:T(8,128)S(1)} %copy.12), channel_id=1, source_target_pairs={{0,2},{2,4},{4,6},{6,8},{8,10},{10,12},{12,14},{14,0},{1,3},{3,5},... | collective-permute-start | bytes 786440 | tf_op jit(solution)/shard_map/while/body/eval_jaxpr/ppermute | solution.py:11
  56.4 9.1 %collective-permute-start.1 = (f32[1,128,256]{2,1,0:T(8,128)S(1)}, f32[1,128,256]{2,1,0:T(8,128)S(1)}, u32[]{:S(2)}, u32[]{:S(2)}) collective-permute-start(f32[1,128,256]{2,1,0:T(8,128)S(1)} %get-tuple-element.184), channel_id=1, source_target_pairs={{0,2},{2,4},{4,6},{6,8},{8,10},{10,12},{12,14},{14,0},{1,3},{3,5},... | collective-permute-start | bytes 393224 | tf_op jit(solution)/shard_map/while/body/eval_jaxpr/ppermute | solution.py:11
  56.5 11.8 %collective-permute-start.2 = (f32[1,128,256]{2,1,0:T(8,128)S(1)}, f32[1,128,256]{2,1,0:T(8,128)S(1)}, u32[]{:S(2)}, u32[]{:S(2)}) collective-permute-start(f32[1,128,256]{2,1,0:T(8,128)S(1)} %get-tuple-element.185), channel_id=1, source_target_pairs={{0,2},{2,4},{4,6},{6,8},{8,10},{10,12},{12,14},{14,0},{1,3},{3,5},... | collective-permute-start | bytes 393224 | tf_op jit(solution)/shard_map/while/body/eval_jaxpr/ppermute | solution.py:11
  57.7 12.8 %collective-permute-start.3 = (f32[1,128,256]{2,1,0:T(8,128)S(1)}, f32[1,128,256]{2,1,0:T(8,128)S(1)}, u32[]{:S(2)}, u32[]{:S(2)}) collective-permute-start(f32[1,128,256]{2,1,0:T(8,128)S(1)} %get-tuple-element.186), channel_id=1, source_target_pairs={{0,2},{2,4},{4,6},{6,8},{8,10},{10,12},{12,14},{14,0},{1,3},{3,5},... | collective-permute-start | bytes 393224 | tf_op jit(solution)/shard_map/while/body/eval_jaxpr/ppermute | solution.py:11
  70.6 20.3 %collective-permute-start = (f32[1,2,128,256]{3,2,1,0:T(8,128)S(1)}, f32[1,2,128,256]{3,2,1,0:T(8,128)S(1)}, u32[]{:S(2)}, u32[]{:S(2)}) collective-permute-start(f32[1,2,128,256]{3,2,1,0:T(8,128)S(1)} %copy.12), channel_id=1, source_target_pairs={{0,2},{2,4},{4,6},{6,8},{8,10},{10,12},{12,14},{14,0},{1,3},{3,5},... | collective-permute-start | bytes 786440 | tf_op jit(solution)/shard_map/while/body/eval_jaxpr/ppermute | solution.py:11
  76.8 9.1 %collective-permute-start.1 = (f32[1,128,256]{2,1,0:T(8,128)S(1)}, f32[1,128,256]{2,1,0:T(8,128)S(1)}, u32[]{:S(2)}, u32[]{:S(2)}) collective-permute-start(f32[1,128,256]{2,1,0:T(8,128)S(1)} %get-tuple-element.184), channel_id=1, source_target_pairs={{0,2},{2,4},{4,6},{6,8},{8,10},{10,12},{12,14},{14,0},{1,3},{3,5},... | collective-permute-start | bytes 393224 | tf_op jit(solution)/shard_map/while/body/eval_jaxpr/ppermute | solution.py:11
  76.8 11.8 %collective-permute-start.2 = (f32[1,128,256]{2,1,0:T(8,128)S(1)}, f32[1,128,256]{2,1,0:T(8,128)S(1)}, u32[]{:S(2)}, u32[]{:S(2)}) collective-permute-start(f32[1,128,256]{2,1,0:T(8,128)S(1)} %get-tuple-element.185), channel_id=1, source_target_pairs={{0,2},{2,4},{4,6},{6,8},{8,10},{10,12},{12,14},{14,0},{1,3},{3,5},... | collective-permute-start | bytes 393224 | tf_op jit(solution)/shard_map/while/body/eval_jaxpr/ppermute | solution.py:11
  76.9 14.0 %collective-permute-start.3 = (f32[1,128,256]{2,1,0:T(8,128)S(1)}, f32[1,128,256]{2,1,0:T(8,128)S(1)}, u32[]{:S(2)}, u32[]{:S(2)}) collective-permute-start(f32[1,128,256]{2,1,0:T(8,128)S(1)} %get-tuple-element.186), channel_id=1, source_target_pairs={{0,2},{2,4},{4,6},{6,8},{8,10},{10,12},{12,14},{14,0},{1,3},{3,5},... | collective-permute-start | bytes 393224 | tf_op jit(solution)/shard_map/while/body/eval_jaxpr/ppermute | solution.py:11
  91.0 20.3 %collective-permute-start = (f32[1,2,128,256]{3,2,1,0:T(8,128)S(1)}, f32[1,2,128,256]{3,2,1,0:T(8,128)S(1)}, u32[]{:S(2)}, u32[]{:S(2)}) collective-permute-start(f32[1,2,128,256]{3,2,1,0:T(8,128)S(1)} %copy.12), channel_id=1, source_target_pairs={{0,2},{2,4},{4,6},{6,8},{8,10},{10,12},{12,14},{14,0},{1,3},{3,5},... | collective-permute-start | bytes 786440 | tf_op jit(solution)/shard_map/while/body/eval_jaxpr/ppermute | solution.py:11
  97.1 9.1 %collective-permute-start.1 = (f32[1,128,256]{2,1,0:T(8,128)S(1)}, f32[1,128,256]{2,1,0:T(8,128)S(1)}, u32[]{:S(2)}, u32[]{:S(2)}) collective-permute-start(f32[1,128,256]{2,1,0:T(8,128)S(1)} %get-tuple-element.184), channel_id=1, source_target_pairs={{0,2},{2,4},{4,6},{6,8},{8,10},{10,12},{12,14},{14,0},{1,3},{3,5},... | collective-permute-start | bytes 393224 | tf_op jit(solution)/shard_map/while/body/eval_jaxpr/ppermute | solution.py:11
  97.2 11.8 %collective-permute-start.2 = (f32[1,128,256]{2,1,0:T(8,128)S(1)}, f32[1,128,256]{2,1,0:T(8,128)S(1)}, u32[]{:S(2)}, u32[]{:S(2)}) collective-permute-start(f32[1,128,256]{2,1,0:T(8,128)S(1)} %get-tuple-element.185), channel_id=1, source_target_pairs={{0,2},{2,4},{4,6},{6,8},{8,10},{10,12},{12,14},{14,0},{1,3},{3,5},... | collective-permute-start | bytes 393224 | tf_op jit(solution)/shard_map/while/body/eval_jaxpr/ppermute | solution.py:11
  97.2 14.0 %collective-permute-start.3 = (f32[1,128,256]{2,1,0:T(8,128)S(1)}, f32[1,128,256]{2,1,0:T(8,128)S(1)}, u32[]{:S(2)}, u32[]{:S(2)}) collective-permute-start(f32[1,128,256]{2,1,0:T(8,128)S(1)} %get-tuple-element.186), channel_id=1, source_target_pairs={{0,2},{2,4},{4,6},{6,8},{8,10},{10,12},{12,14},{14,0},{1,3},{3,5},... | collective-permute-start | bytes 393224 | tf_op jit(solution)/shard_map/while/body/eval_jaxpr/ppermute | solution.py:11
  111.3 20.3 %collective-permute-start = (f32[1,2,128,256]{3,2,1,0:T(8,128)S(1)}, f32[1,2,128,256]{3,2,1,0:T(8,128)S(1)}, u32[]{:S(2)}, u32[]{:S(2)}) collective-permute-start(f32[1,2,128,256]{3,2,1,0:T(8,128)S(1)} %copy.12), channel_id=1, source_target_pairs={{0,2},{2,4},{4,6},{6,8},{8,10},{10,12},{12,14},{14,0},{1,3},{3,5},... | collective-permute-start | bytes 786440 | tf_op jit(solution)/shard_map/while/body/eval_jaxpr/ppermute | solution.py:11
  117.5 9.1 %collective-permute-start.1 = (f32[1,128,256]{2,1,0:T(8,128)S(1)}, f32[1,128,256]{2,1,0:T(8,128)S(1)}, u32[]{:S(2)}, u32[]{:S(2)}) collective-permute-start(f32[1,128,256]{2,1,0:T(8,128)S(1)} %get-tuple-element.184), channel_id=1, source_target_pairs={{0,2},{2,4},{4,6},{6,8},{8,10},{10,12},{12,14},{14,0},{1,3},{3,5},... | collective-permute-start | bytes 393224 | tf_op jit(solution)/shard_map/while/body/eval_jaxpr/ppermute | solution.py:11
  117.5 11.8 %collective-permute-start.2 = (f32[1,128,256]{2,1,0:T(8,128)S(1)}, f32[1,128,256]{2,1,0:T(8,128)S(1)}, u32[]{:S(2)}, u32[]{:S(2)}) collective-permute-start(f32[1,128,256]{2,1,0:T(8,128)S(1)} %get-tuple-element.185), channel_id=1, source_target_pairs={{0,2},{2,4},{4,6},{6,8},{8,10},{10,12},{12,14},{14,0},{1,3},{3,5},... | collective-permute-start | bytes 393224 | tf_op jit(solution)/shard_map/while/body/eval_jaxpr/ppermute | solution.py:11
  117.6 14.0 %collective-permute-start.3 = (f32[1,128,256]{2,1,0:T(8,128)S(1)}, f32[1,128,256]{2,1,0:T(8,128)S(1)}, u32[]{:S(2)}, u32[]{:S(2)}) collective-permute-start(f32[1,128,256]{2,1,0:T(8,128)S(1)} %get-tuple-element.186), channel_id=1, source_target_pairs={{0,2},{2,4},{4,6},{6,8},{8,10},{10,12},{12,14},{14,0},{1,3},{3,5},... | collective-permute-start | bytes 393224 | tf_op jit(solution)/shard_map/while/body/eval_jaxpr/ppermute | solution.py:11
  131.7 20.3 %collective-permute-start = (f32[1,2,128,256]{3,2,1,0:T(8,128)S(1)}, f32[1,2,128,256]{3,2,1,0:T(8,128)S(1)}, u32[]{:S(2)}, u32[]{:S(2)}) collective-permute-start(f32[1,2,128,256]{3,2,1,0:T(8,128)S(1)} %copy.12), channel_id=1, source_target_pairs={{0,2},{2,4},{4,6},{6,8},{8,10},{10,12},{12,14},{14,0},{1,3},{3,5},... | collective-permute-start | bytes 786440 | tf_op jit(solution)/shard_map/while/body/eval_jaxpr/ppermute | solution.py:11
  137.8 9.1 %collective-permute-start.1 = (f32[1,128,256]{2,1,0:T(8,128)S(1)}, f32[1,128,256]{2,1,0:T(8,128)S(1)}, u32[]{:S(2)}, u32[]{:S(2)}) collective-permute-start(f32[1,128,256]{2,1,0:T(8,128)S(1)} %get-tuple-element.184), channel_id=1, source_target_pairs={{0,2},{2,4},{4,6},{6,8},{8,10},{10,12},{12,14},{14,0},{1,3},{3,5},... | collective-permute-start | bytes 393224 | tf_op jit(solution)/shard_map/while/body/eval_jaxpr/ppermute | solution.py:11
  137.9 11.8 %collective-permute-start.2 = (f32[1,128,256]{2,1,0:T(8,128)S(1)}, f32[1,128,256]{2,1,0:T(8,128)S(1)}, u32[]{:S(2)}, u32[]{:S(2)}) collective-permute-start(f32[1,128,256]{2,1,0:T(8,128)S(1)} %get-tuple-element.185), channel_id=1, source_target_pairs={{0,2},{2,4},{4,6},{6,8},{8,10},{10,12},{12,14},{14,0},{1,3},{3,5},... | collective-permute-start | bytes 393224 | tf_op jit(solution)/shard_map/while/body/eval_jaxpr/ppermute | solution.py:11
  138.0 14.0 %collective-permute-start.3 = (f32[1,128,256]{2,1,0:T(8,128)S(1)}, f32[1,128,256]{2,1,0:T(8,128)S(1)}, u32[]{:S(2)}, u32[]{:S(2)}) collective-permute-start(f32[1,128,256]{2,1,0:T(8,128)S(1)} %get-tuple-element.186), channel_id=1, source_target_pairs={{0,2},{2,4},{4,6},{6,8},{8,10},{10,12},{12,14},{14,0},{1,3},{3,5},... | collective-permute-start | bytes 393224 | tf_op jit(solution)/shard_map/while/body/eval_jaxpr/ppermute | solution.py:11
  152.0 20.3 %collective-permute-start = (f32[1,2,128,256]{3,2,1,0:T(8,128)S(1)}, f32[1,2,128,256]{3,2,1,0:T(8,128)S(1)}, u32[]{:S(2)}, u32[]{:S(2)}) collective-permute-start(f32[1,2,128,256]{3,2,1,0:T(8,128)S(1)} %copy.12), channel_id=1, source_target_pairs={{0,2},{2,4},{4,6},{6,8},{8,10},{10,12},{12,14},{14,0},{1,3},{3,5},... | collective-permute-start | bytes 786440 | tf_op jit(solution)/shard_map/while/body/eval_jaxpr/ppermute | solution.py:11
  158.2 9.1 %collective-permute-start.1 = (f32[1,128,256]{2,1,0:T(8,128)S(1)}, f32[1,128,256]{2,1,0:T(8,128)S(1)}, u32[]{:S(2)}, u32[]{:S(2)}) collective-permute-start(f32[1,128,256]{2,1,0:T(8,128)S(1)} %get-tuple-element.184), channel_id=1, source_target_pairs={{0,2},{2,4},{4,6},{6,8},{8,10},{10,12},{12,14},{14,0},{1,3},{3,5},... | collective-permute-start | bytes 393224 | tf_op jit(solution)/shard_map/while/body/eval_jaxpr/ppermute | solution.py:11
  158.2 11.8 %collective-permute-start.2 = (f32[1,128,256]{2,1,0:T(8,128)S(1)}, f32[1,128,256]{2,1,0:T(8,128)S(1)}, u32[]{:S(2)}, u32[]{:S(2)}) collective-permute-start(f32[1,128,256]{2,1,0:T(8,128)S(1)} %get-tuple-element.185), channel_id=1, source_target_pairs={{0,2},{2,4},{4,6},{6,8},{8,10},{10,12},{12,14},{14,0},{1,3},{3,5},... | collective-permute-start | bytes 393224 | tf_op jit(solution)/shard_map/while/body/eval_jaxpr/ppermute | solution.py:11
  158.3 14.0 %collective-permute-start.3 = (f32[1,128,256]{2,1,0:T(8,128)S(1)}, f32[1,128,256]{2,1,0:T(8,128)S(1)}, u32[]{:S(2)}, u32[]{:S(2)}) collective-permute-start(f32[1,128,256]{2,1,0:T(8,128)S(1)} %get-tuple-element.186), channel_id=1, source_target_pairs={{0,2},{2,4},{4,6},{6,8},{8,10},{10,12},{12,14},{14,0},{1,3},{3,5},... | collective-permute-start | bytes 393224 | tf_op jit(solution)/shard_map/while/body/eval_jaxpr/ppermute | solution.py:11
  (3 other events, 2.9 us)
where the time goes:
time: 174 us
  waiting for transfers between devices  96.4 us (55%)
  matrix products  31 us (18%)
  starting transfers between devices  20 us (11%)
  blocking collectives  19.7 us (11%)
  local copies, waits for them, and re-layouts  2.67 us (2%)
  other arithmetic  2.11 us (1%)
    ppermute x32, waiting for transfers between devices, shifted(): return lax.ppermute(x, axis, [(i, (i + by) % peers) for i in range(peers)])  96.4 us
    ppermute x32, starting transfers between devices, shifted(): return lax.ppermute(x, axis, [(i, (i + by) % peers) for i in range(peers)])  20 us
    all_gather x8, blocking collectives, visit(): full = lax.all_gather(held, 'tile', axis=2, tiled=True)  17.4 us
    dot_general x8, matrix products, correlate(): jnp.einsum('nyk,kx->nyx', along_imag, col_sin, precision=highest)  10.5 us
    dot_general x8, matrix products, correlate(): maps = jnp.einsum('nyk,kx->nyx', along_real, col_cos, precision=highest)  10.4 us
    dot_general x8, matrix products, correlate(): jnp.einsum('yk,nkx->nyx', row_table, real_part, precision=highest)  5.05 us
    dot_general x8, matrix products, correlate(): jnp.einsum('yk,nkx->nyx', row_table, imag_part, precision=highest)  5.05 us
  transfers between devices with their start and end apart: 32, of which 24 were waited for; matrix products, arithmetic and copies ran while one was open for 18% of the time, Pallas kernels for 0%

commit v1 on v0

v1 whole, which is shorter than its diff:
```python
import math

import jax
import jax.numpy as jnp
import ml_dtypes
import numpy as np
from jax import lax
from jax.experimental import pallas as pl
from jax.experimental.pallas import tpu as pltpu
from jax.sharding import PartitionSpec as P

MESH = pl.DeviceIdType.MESH
BF16 = jnp.bfloat16
F32 = jnp.float32


def two_parts(table):
    high = table.astype(np.float32).astype(ml_dtypes.bfloat16)
    low = (table - high.astype(np.float64)).astype(np.float32).astype(ml_dtypes.bfloat16)
    return np.stack([high, low])


def tables(side):
    freq = np.arange(side)
    angle = (freq[:, None] * freq[None, :] % side) * (2.0 * math.pi / side)
    cos, sin = np.cos(angle), np.sin(angle)
    rows = np.concatenate([np.concatenate([cos, -sin], 1), np.concatenate([-sin, -cos], 1)], 0)
    cols = np.concatenate([cos, sin], 0)
    return two_parts(rows), two_parts(cols)


def split(value):
    high = value.astype(BF16)
    return high, (value - high.astype(F32)).astype(BF16)


def dot(left, right):
    return jnp.dot(left, right, preferred_element_type=F32)


def correlator(side, count, pieces, white, z_parts, y_parts, row_ref, col_ref, stats):
    half = side // 2
    chunk = 64

    def one(template, first):
        square = jnp.zeros((8, side), F32)
        for at in range(0, side, chunk):
            h, row = at // half, at % half
            real = template.at[0, h][row : row + chunk]
            imag = template.at[1, h][row : row + chunk]
            s_real = white[0, at : at + chunk]
            s_imag = white[1, at : at + chunk]
            square = square + jnp.sum((real * real + imag * imag).reshape(chunk // 8, 8, side), 0)
            z_parts[0, at : at + chunk], z_parts[1, at : at + chunk] = split(s_real * real + s_imag * imag)
            below = slice(side + at, side + at + chunk)
            z_parts[0, below], z_parts[1, below] = split(s_imag * real - s_real * imag)
        power = jnp.sum(square, axis=(0, 1), keepdims=True) / (2.0 * side * side)
        factor = 1.0 / (jnp.sqrt(power + 1e-06) * side)
        for block in range(4):
            rows = slice(block * half, (block + 1) * half)
            part = dot(row_ref[0, rows], z_parts[0]) + dot(row_ref[0, rows], z_parts[1])
            part = part + dot(row_ref[1, rows], z_parts[0])
            to = slice((block % 2) * half, (block % 2 + 1) * half)
            lanes = slice((block // 2) * side, (block // 2 + 1) * side)
            y_parts[0, to, lanes], y_parts[1, to, lanes] = split(part)
        for block in range(2):
            rows = slice(block * half, (block + 1) * half)
            maps = dot(y_parts[0, rows], col_ref[0]) + dot(y_parts[1, rows], col_ref[0])
            maps = (maps + dot(y_parts[0, rows], col_ref[1])) * factor
            if first:
                stats[0, block] = maps
                stats[1, block] = maps
                stats[2, block] = maps * maps
            else:
                stats[0, block] = jnp.maximum(stats[0, block], maps)
                stats[1, block] += maps
                stats[2, block] += maps * maps

    return one


def kernel(side, count, spectra_ref, template_ref, weight_ref, row_ref, col_ref, peak_ref, mean_ref, square_ref,
           slots, spectrum, white, z_parts, y_parts, stats, other_stats,
           first_sem, pass_sem, piece_sem, spectrum_sem, stats_sem):
    half = side // 2
    x, orient, core = lax.axis_index("groups"), lax.axis_index("orient"), lax.axis_index("tile")
    y, z = orient % 2, orient // 2
    interior = jnp.logical_and(z > 0, z < 3)

    def chip(cx, cy, cz, c):
        return {"groups": cx, "orient": cz * 2 + cy, "tile": c}

    barrier = pltpu.get_barrier_semaphore()

    def greet(where):
        pl.semaphore_signal(barrier, inc=1, device_id=where, device_id_type=MESH)

    greet(chip(x, y, z, 1 - core))
    greet(chip(1 - x, y, z, core))
    for c in range(2):
        greet(chip(x, 1 - y, z, c))

    @pl.when(z > 0)
    def _():
        for c in range(2):
            greet(chip(x, y, z - 1, c))

    @pl.when(z < 3)
    def _():
        for c in range(2):
            greet(chip(x, y, z + 1, c))

    @pl.when(interior)
    def _():
        pl.semaphore_wait(barrier, 8)

    @pl.when(jnp.logical_not(interior))
    def _():
        pl.semaphore_wait(barrier, 6)

    home = (y + z) % 2

    def first_copy(p, way, where):
        return pltpu.make_async_remote_copy(
            src_ref=template_ref.at[0, p],
            dst_ref=slots.at[z, p, core],
            send_sem=first_sem.at[way, p],
            recv_sem=piece_sem.at[z, p, core],
            device_id=where,
            device_id_type=MESH,
        )

    def stay(p):
        return pltpu.make_async_copy(template_ref.at[0, p], slots.at[z, p, core], piece_sem.at[z, p, core])

    up, down = chip(x, y, z + 1, home), chip(x, y, z - 1, home)
    across, sibling = chip(x, 1 - y, z, home), chip(x, y, z, home)
    spectrum_copy = pltpu.make_async_remote_copy(
        src_ref=spectra_ref.at[0],
        dst_ref=spectrum,
        send_sem=spectrum_sem.at[0],
        recv_sem=spectrum_sem.at[1],
        device_id=chip(x, y, z, 1 - core),
        device_id_type=MESH,
    )
    for p in range(2):

        @pl.when(z < 3)
        def _():
            first_copy(p, 0, up).start()

        @pl.when(z > 0)
        def _():
            first_copy(p, 1, down).start()

        first_copy(p, 2, across).start()
    spectrum_copy.start()
    for p in range(2):

        @pl.when(home != core)
        def _():
            first_copy(p, 3, sibling).start()

        @pl.when(home == core)
        def _():
            stay(p).start()

    def arrived(s, p, h):
        ref = slots.at[s, p, h]
        pltpu.make_async_remote_copy(
            src_ref=ref, dst_ref=ref, send_sem=spectrum_sem.at[0], recv_sem=piece_sem.at[s, p, h],
            device_id=sibling, device_id_type=MESH,
        ).wait_recv()

    order = (z + 1 - 2 * (z % 2), 2 - z // 2, 3 - 3 * (z // 2))
    away = (3 - z, 3 * (z // 2), 3 * (z // 2))

    def pass_copy(k, p, way, where):
        ref = slots.at[order[k], p, x]
        return pltpu.make_async_remote_copy(
            src_ref=ref, dst_ref=ref, send_sem=pass_sem.at[k, p, way], recv_sem=piece_sem.at[order[k], p, x],
            device_id=where, device_id_type=MESH,
        )

    def passes(k, p):
        in_column = (core + order[k]) % 2 == y
        if k == 0:
            over = jnp.logical_not(in_column)
        elif k == 1:
            over = jnp.logical_not(jnp.logical_and(in_column, interior))
        else:
            over = None
        return (
            (jnp.logical_and(interior, in_column), pass_copy(k, p, 0, chip(x, y, away[k], core))),
            (in_column, pass_copy(k, p, 1, chip(x, 1 - y, z, core))),
            (over, pass_copy(k, p, 2, chip(1 - x, y, z, core))),
        )

    def hand_on(k):
        for p in range(2):
            arrived(order[k], p, x)
            for condition, copy in passes(k, p):
                if condition is None:
                    copy.start()
                else:
                    pl.when(condition)(copy.start)

    one = correlator(side, count, None, white, z_parts, y_parts, row_ref, col_ref, stats)

    spectrum_copy.wait_recv()
    for p in range(2):
        mine = pl.ds(pl.multiple_of(core * half, half), half)
        theirs = pl.ds(pl.multiple_of((1 - core) * half, half), half)
        white[p, mine] = spectra_ref[0, p] * weight_ref[mine]
        white[p, theirs] = spectrum[p] * weight_ref[theirs]

    hand_on(0)
    for p in range(2):
        for h in range(2):
            arrived(z, p, h)
    one(slots.at[z], True)
    hand_on(1)
    for k in range(3):
        for p in range(2):
            arrived(order[k], p, 1 - x)
        one(slots.at[order[k]], False)
        if k == 0:
            hand_on(2)

    stats_copy = [
        pltpu.make_async_remote_copy(
            src_ref=stats.at[i, 1 - core],
            dst_ref=other_stats.at[i],
            send_sem=stats_sem.at[0, i],
            recv_sem=stats_sem.at[1, i],
            device_id=chip(x, y, z, 1 - core),
            device_id_type=MESH,
        )
        for i in range(3)
    ]
    for copy in stats_copy:
        copy.start()
    stats_copy[0].wait_recv()
    peak_ref[0] = jnp.maximum(stats[0, core], other_stats[0])
    stats_copy[1].wait_recv()
    mean_ref[0] = (stats[1, core] + other_stats[1]) / count
    stats_copy[2].wait_recv()
    square_ref[0] = (stats[2, core] + other_stats[2]) / count

    for copy in stats_copy:
        copy.wait_send()
    spectrum_copy.wait_send()
    for p in range(2):

        @pl.when(z < 3)
        def _():
            first_copy(p, 0, up).wait_send()

        @pl.when(z > 0)
        def _():
            first_copy(p, 1, down).wait_send()

        first_copy(p, 2, across).wait_send()

        @pl.when(home != core)
        def _():
            first_copy(p, 3, sibling).wait_send()

        for k in range(3):
            for condition, copy in passes(k, p):
                if condition is None:
                    copy.wait_send()
                else:
                    pl.when(condition)(copy.wait_send)


def on_box(spectra, templates, weights):
    side, half = spectra.shape[3], spectra.shape[2]
    count = lax.axis_size("orient") * templates.shape[0]
    rows, cols = tables(side)
    out = jax.ShapeDtypeStruct((1, half, side), F32)

    def body(*refs):
        kernel(side, count, *refs)

    vmem = pl.BlockSpec(memory_space=pltpu.VMEM)
    return pl.pallas_call(
        body,
        out_shape=(out, out, out),
        in_specs=[vmem] * 5,
        out_specs=(vmem, vmem, vmem),
        scratch_shapes=[
            pltpu.VMEM((4, 2, 2, half, side), F32),
            pltpu.VMEM((2, half, side), F32),
            pltpu.VMEM((2, side, side), F32),
            pltpu.VMEM((2, 2 * side, side), BF16),
            pltpu.VMEM((2, side, 2 * side), BF16),
            pltpu.VMEM((3, 2, half, side), F32),
            pltpu.VMEM((3, half, side), F32),
            pltpu.SemaphoreType.DMA((4, 2)),
            pltpu.SemaphoreType.DMA((3, 2, 3)),
            pltpu.SemaphoreType.DMA((4, 2, 2)),
            pltpu.SemaphoreType.DMA((2,)),
            pltpu.SemaphoreType.DMA((2, 3)),
        ],
        compiler_params=pltpu.CompilerParams(
            collective_id=0, has_side_effects=True, vmem_limit_bytes=48 * 1024 * 1024
        ),
    )(spectra, templates, weights, jnp.asarray(rows), jnp.asarray(cols))


def twiddle(rows, cols, side):
    phase = rows[:, None] * cols[None, :] % side
    angle = phase.astype(F32) * (2.0 * math.pi / side)
    return (jnp.cos(angle), jnp.sin(angle))


def on_any(spectra, templates, weights):
    side, half = spectra.shape[3], spectra.shape[2]
    count = lax.axis_size("orient") * templates.shape[0]
    out_rows = lax.axis_index("tile") * half + lax.iota(jnp.int32, half)
    freq = lax.iota(jnp.int32, side)
    row_cos, row_sin = twiddle(out_rows, freq, side)
    col_cos, col_sin = twiddle(freq, freq, side)
    row_table = jnp.concatenate([row_cos, row_sin], 0)
    highest = lax.Precision.HIGHEST
    pieces = lax.all_gather(templates, ("orient",), axis=0, tiled=True)
    pieces = lax.all_gather(pieces, "tile", axis=2, tiled=True)
    full = lax.all_gather(spectra, "tile", axis=2, tiled=True)

    def one_orientation(carry, template):
        template = template / jnp.sqrt(jnp.mean(template * template) + 1e-06)
        real_part = (full[:, 0] * template[0] + full[:, 1] * template[1]) * weights
        imag_part = (full[:, 1] * template[0] - full[:, 0] * template[1]) * weights
        stack_real = jnp.einsum("yk,nkx->nyx", row_table, real_part, precision=highest)
        stack_imag = jnp.einsum("yk,nkx->nyx", row_table, imag_part, precision=highest)
        along_real = stack_real[:, :half] - stack_imag[:, half:]
        along_imag = stack_imag[:, :half] + stack_real[:, half:]
        maps = jnp.einsum("nyk,kx->nyx", along_real, col_cos, precision=highest)
        maps = (maps - jnp.einsum("nyk,kx->nyx", along_imag, col_sin, precision=highest)) / side
        best, total, squares = carry
        return ((jnp.maximum(best, maps), total + maps, squares + maps * maps), None)

    shape = (spectra.shape[0], half, side)
    initial = (jnp.full(shape, -jnp.inf, F32), jnp.zeros(shape, F32), jnp.zeros(shape, F32))
    (best, total, squares), _ = lax.scan(one_orientation, initial, pieces)
    return (best, total / count, squares / count)


def solution(mesh):
    box = dict(mesh.shape) == {"groups": 2, "orient": 8, "tile": 2}
    in_specs = (
        P(("groups", "orient"), None, "tile", None),
        P("orient", None, "tile", None),
        P("groups", None),
    )
    out_specs = (P(("groups", "orient"), "tile", None),) * 3
    body = on_box if box else on_any
    return jax.shard_map(body, mesh=mesh, in_specs=in_specs, out_specs=out_specs, check_vma=False)
```

time: 174 us -> 44.1 us (0.25)
  waiting for transfers between devices: 96.4 us -> 0 us
  Pallas kernels: 0 us -> 36.1 us
  matrix products: 31 us -> 0 us
  starting transfers between devices: 20 us -> 0 us
  blocking collectives: 19.7 us -> 0 us
  local copies, waits for them, and re-layouts: 2.67 us -> 7.08 us
  other arithmetic: 2.11 us -> 0 us
    ppermute x32 -> x0, waiting for transfers between devices: 96.4 us -> none  [shifted(): return lax.ppermute(x, axis, [(i, (i + by) % peers) for i in range(peers)])]
    pallas_call x0 -> x1, Pallas kernels: none -> 36.1 us  [on_box(): pl.pallas_call(body, out_shape=(out, out, out), in_specs=[vmem] * 5, out_...]
    dot_general x32 -> x0, matrix products: 31 us -> none  [the longest x8 10.5 us: correlate(): jnp.einsum('nyk,kx->nyx', along_imag, col_sin, precision=highest)]
    ppermute x32 -> x0, starting transfers between devices: 20 us -> none  [shifted(): return lax.ppermute(x, axis, [(i, (i + by) % peers) for i in range(peers)])]
    all_gather x9 -> x0, blocking collectives: 19.7 us -> none  [the longest x8 17.4 us: visit(): full = lax.all_gather(held, 'tile', axis=2, tiled=True)]
    unnamed x7 -> x13, local copies, waits for them, and re-layouts: 2.5 us -> 7.08 us
  transfers between devices with their start and end apart: 32 -> 0, of which waited for: 24 -> 0; matrix products, arithmetic and copies ran while one was open for 18% -> 0% of each run, Pallas kernels for 0% -> 0%
where the time goes in v1:
time: 44.1 us; the launch traced here: 43.9 us
  Pallas kernels  36.1 us (82%)
  local copies, waits for them, and re-layouts  7.08 us (16%)
  between operations  0.65 us (1%)
    pallas_call x1, Pallas kernels, on_box(): pl.pallas_call(body, out_shape=(out, out, out), in_specs=[vmem] * 5, out_...  36.1 us
    unnamed x13, local copies, waits for them, and re-layouts  7.08 us

profile of v1, /device:TPU:0, one launch (start us, length us, event | category | flops | bytes accessed | tf_op | source)
XLA Modules:
  0.0 43.9 jit_solution(9939960048706828736)
XLA Ops:
  0.6 0.0 copy-start
  0.6 1.2 %copy-done = bf16[2,512,512]{2,1,0:T(8,128)(2,1)S(1)} copy-done((bf16[2,512,512]{2,1,0:T(8,128)(2,1)S(1)}, bf16[2,512,512]{2,1,0:T(8,128)(2,1)}, u32[]{:S(2)}) %copy-start) | copy-done | bytes 1048600
  1.9 0.0 copy-start.1
  1.9 1.0 %copy-done.1 = bf16[2,512,256]{2,1,0:T(8,128)(2,1)S(1)} copy-done((bf16[2,512,256]{2,1,0:T(8,128)(2,1)S(1)}, bf16[2,512,256]{2,1,0:T(8,128)(2,1)}, u32[]{:S(2)}) %copy-start.1) | copy-done | bytes 524312
  2.9 0.0 copy-start.2
  2.9 0.9 %copy-done.2 = f32[1,2,128,256]{3,2,1,0:T(8,128)S(1)} copy-done((f32[1,2,128,256]{3,2,1,0:T(8,128)S(1)}, f32[1,2,128,256]{3,2,1,0:T(8,128)}, u32[]{:S(2)}) %copy-start.2) | copy-done | bytes 262168
  3.9 0.0 copy-start.3
  3.9 0.9 %copy-done.3 = f32[1,2,128,256]{3,2,1,0:T(8,128)S(1)} copy-done((f32[1,2,128,256]{3,2,1,0:T(8,128)S(1)}, f32[1,2,128,256]{3,2,1,0:T(8,128)}, u32[]{:S(2)}) %copy-start.3) | copy-done | bytes 262168
  4.8 0.0 copy-start.4
  4.8 0.9 %copy-done.4 = f32[256,256]{1,0:T(8,128)S(1)} copy-done((f32[256,256]{1,0:T(8,128)S(1)}, f32[256,256]{1,0:T(8,128)}, u32[]{:S(2)}) %copy-start.4) | copy-done | bytes 262168
  5.8 36.1 %shard_map.76 = (f32[1,128,256]{2,1,0:T(8,128)S(1)}, f32[1,128,256]{2,1,0:T(8,128)S(1)}, f32[1,128,256]{2,1,0:T(8,128)S(1)}) custom-call(f32[1,2,128,256]{3,2,1,0:T(8,128)S(1)} %copy-done.2, f32[1,2,128,256]{3,2,1,0:T(8,128)S(1)} %copy-done.3, f32[256,256]{1,0:T(8,128)S(1)} %copy-done.4, bf16[2,512,512]{2,1,0:T(8,128)(2,1)S(1)} %copy-done, ...), custom_call_target="tpu_custom_call" | custom-call | tf_op jit(solution)/shard_map/pallas_call | solution.py:287
  41.9 0.7 %copy.11 = f32[1,128,256]{2,1,0:T(8,128)} copy(f32[1,128,256]{2,1,0:T(8,128)S(1)} %get-tuple-element.6) | data formatting | bytes 262144
  42.5 0.7 %copy.12 = f32[1,128,256]{2,1,0:T(8,128)} copy(f32[1,128,256]{2,1,0:T(8,128)S(1)} %get-tuple-element.7) | data formatting | bytes 262144
  43.2 0.7 %copy.13 = f32[1,128,256]{2,1,0:T(8,128)} copy(f32[1,128,256]{2,1,0:T(8,128)S(1)} %get-tuple-element.8) | data formatting | bytes 262144
Async XLA Ops:
  0.6 1.2 %copy-start = (bf16[2,512,512]{2,1,0:T(8,128)(2,1)S(1)}, bf16[2,512,512]{2,1,0:T(8,128)(2,1)}, u32[]{:S(2)}) copy-start(bf16[2,512,512]{2,1,0:T(8,128)(2,1)} %constant.4.clone.refs_3_) | copy-start | bytes 3145732
  1.9 1.0 %copy-start.1 = (bf16[2,512,256]{2,1,0:T(8,128)(2,1)S(1)}, bf16[2,512,256]{2,1,0:T(8,128)(2,1)}, u32[]{:S(2)}) copy-start(bf16[2,512,256]{2,1,0:T(8,128)(2,1)} %constant.5.clone.refs_4_) | copy-start | bytes 1572868
  2.9 0.9 %copy-start.2 = (f32[1,2,128,256]{3,2,1,0:T(8,128)S(1)}, f32[1,2,128,256]{3,2,1,0:T(8,128)}, u32[]{:S(2)}) copy-start(f32[1,2,128,256]{3,2,1,0:T(8,128)} %refs_0_.1) | copy-start | bytes 786436
  3.9 0.9 %copy-start.3 = (f32[1,2,128,256]{3,2,1,0:T(8,128)S(1)}, f32[1,2,128,256]{3,2,1,0:T(8,128)}, u32[]{:S(2)}) copy-start(f32[1,2,128,256]{3,2,1,0:T(8,128)} %refs_1_.1) | copy-start | bytes 786436
  4.8 0.9 %copy-start.4 = (f32[256,256]{1,0:T(8,128)S(1)}, f32[256,256]{1,0:T(8,128)}, u32[]{:S(2)}) copy-start(f32[256,256]{1,0:T(8,128)} %refs_2_.1) | copy-start | bytes 786436

commit v2 on v1

--- a/solution.py
+++ b/solution.py
@@ -40,14 +40,14 @@
 
 def correlator(side, count, pieces, white, z_parts, y_parts, row_ref, col_ref, stats):
     half = side // 2
-    chunk = 64
+    chunk = half // 2
 
     def one(template, first):
         square = jnp.zeros((8, side), F32)
         for at in range(0, side, chunk):
             h, row = at // half, at % half
-            real = template.at[0, h][row : row + chunk]
-            imag = template.at[1, h][row : row + chunk]
+            real = template[0, h, row // chunk]
+            imag = template[1, h, row // chunk]
             s_real = white[0, at : at + chunk]
             s_imag = white[1, at : at + chunk]
             square = square + jnp.sum((real * real + imag * imag).reshape(chunk // 8, 8, side), 0)
@@ -79,9 +79,9 @@
     return one
 
 
-def kernel(side, count, spectra_ref, template_ref, weight_ref, row_ref, col_ref, peak_ref, mean_ref, square_ref,
-           slots, spectrum, white, z_parts, y_parts, stats, other_stats,
-           first_sem, pass_sem, piece_sem, spectrum_sem, stats_sem):
+def kernel(side, count, spectra_ref, template_ref, weight_ref, row_ref, col_ref, out_ref,
+           slots, spectrum, weight, row_table, col_table, white, z_parts, y_parts, stats, other_stats,
+           first_sem, pass_sem, piece_sem, spectrum_sem, stats_sem, load_sem):
     half = side // 2
     x, orient, core = lax.axis_index("groups"), lax.axis_index("orient"), lax.axis_index("tile")
     y, z = orient % 2, orient // 2
@@ -90,6 +90,14 @@
     def chip(cx, cy, cz, c):
         return {"groups": cx, "orient": cz * 2 + cy, "tile": c}
 
+    loads = [
+        pltpu.make_async_copy(spectra_ref.at[0], spectrum.at[core], load_sem.at[0]),
+        pltpu.make_async_copy(weight_ref, weight, load_sem.at[1]),
+        pltpu.make_async_copy(row_ref, row_table, load_sem.at[2]),
+        pltpu.make_async_copy(col_ref, col_table, load_sem.at[3]),
+    ]
+    for copy in loads:
+        copy.start()
     barrier = pltpu.get_barrier_semaphore()
 
     def greet(where):
@@ -120,112 +128,116 @@
 
     home = (y + z) % 2
 
-    def first_copy(p, way, where):
+    fine = half // 2
+    pieces = range(4)
+
+    def first_copy(q, way, where):
         return pltpu.make_async_remote_copy(
-            src_ref=template_ref.at[0, p],
-            dst_ref=slots.at[z, p, core],
-            send_sem=first_sem.at[way, p],
-            recv_sem=piece_sem.at[z, p, core],
+            src_ref=template_ref.at[0, q // 2, pl.ds(q % 2 * fine, fine)],
+            dst_ref=slots.at[z, q // 2, core, q % 2],
+            send_sem=first_sem.at[way, q],
+            recv_sem=piece_sem.at[z, core, q],
             device_id=where,
             device_id_type=MESH,
         )
 
-    def stay(p):
-        return pltpu.make_async_copy(template_ref.at[0, p], slots.at[z, p, core], piece_sem.at[z, p, core])
-
-    up, down = chip(x, y, z + 1, home), chip(x, y, z - 1, home)
+    def stay(q):
+        return pltpu.make_async_copy(
+            template_ref.at[0, q // 2, pl.ds(q % 2 * fine, fine)],
+            slots.at[z, q // 2, core, q % 2],
+            piece_sem.at[z, core, q],
+        )
+
+    up, down, far = chip(x, y, z + 1, home), chip(x, y, z - 1, home), chip(x, y, 3 - z, home)
     across, sibling = chip(x, 1 - y, z, home), chip(x, y, z, home)
+    chain = x == core
+
+    def near(q, act):
+        pl.when(z < 3)(lambda: act(first_copy(q, 0, up)))
+        pl.when(z > 0)(lambda: act(first_copy(q, 1, down)))
+
+    def along(act):
+        for q in pieces:
+            near(q, act)
+
+
+    def start(copy):
+        copy.start()
+
+    def sent(copy):
+        copy.wait_send()
+
     spectrum_copy = pltpu.make_async_remote_copy(
         src_ref=spectra_ref.at[0],
-        dst_ref=spectrum,
+        dst_ref=spectrum.at[core],
         send_sem=spectrum_sem.at[0],
         recv_sem=spectrum_sem.at[1],
         device_id=chip(x, y, z, 1 - core),
         device_id_type=MESH,
     )
-    for p in range(2):
-
-        @pl.when(z < 3)
-        def _():
-            first_copy(p, 0, up).start()
-
-        @pl.when(z > 0)
-        def _():
-            first_copy(p, 1, down).start()
-
-        first_copy(p, 2, across).start()
+    for q in pieces:
+        near(q, start)
+        first_copy(q, 2, across).start()
     spectrum_copy.start()
-    for p in range(2):
-
-        @pl.when(home != core)
-        def _():
-            first_copy(p, 3, sibling).start()
-
-        @pl.when(home == core)
-        def _():
-            stay(p).start()
-
-    def arrived(s, p, h):
-        ref = slots.at[s, p, h]
+    for q in pieces:
+        pl.when(home != core)(first_copy(q, 3, sibling).start)
+        pl.when(home == core)(stay(q).start)
+
+
+    def arrived(s, h, q):
+        ref = slots.at[s, q // 2, h, q % 2]
         pltpu.make_async_remote_copy(
-            src_ref=ref, dst_ref=ref, send_sem=spectrum_sem.at[0], recv_sem=piece_sem.at[s, p, h],
+            src_ref=ref, dst_ref=ref, send_sem=spectrum_sem.at[0], recv_sem=piece_sem.at[s, h, q],
             device_id=sibling, device_id_type=MESH,
         ).wait_recv()
 
     order = (z + 1 - 2 * (z % 2), 2 - z // 2, 3 - 3 * (z // 2))
     away = (3 - z, 3 * (z // 2), 3 * (z // 2))
 
-    def pass_copy(k, p, way, where):
-        ref = slots.at[order[k], p, x]
+    def pass_copy(k, q, way, where):
+        ref = slots.at[order[k], q // 2, x, q % 2]
         return pltpu.make_async_remote_copy(
-            src_ref=ref, dst_ref=ref, send_sem=pass_sem.at[k, p, way], recv_sem=piece_sem.at[order[k], p, x],
+            src_ref=ref, dst_ref=ref, send_sem=pass_sem.at[k, q, way], recv_sem=piece_sem.at[order[k], x, q],
             device_id=where, device_id_type=MESH,
         )
 
-    def passes(k, p):
+    def passes(k, act, ready):
         in_column = (core + order[k]) % 2 == y
-        if k == 0:
-            over = jnp.logical_not(in_column)
-        elif k == 1:
-            over = jnp.logical_not(jnp.logical_and(in_column, interior))
-        else:
-            over = None
-        return (
-            (jnp.logical_and(interior, in_column), pass_copy(k, p, 0, chip(x, y, away[k], core))),
-            (in_column, pass_copy(k, p, 1, chip(x, 1 - y, z, core))),
-            (over, pass_copy(k, p, 2, chip(1 - x, y, z, core))),
-        )
+        outside = jnp.logical_not(in_column)
+        over = (outside, jnp.logical_or(outside, jnp.logical_not(interior)), z >= 0)[k]
+        for q in pieces:
+            ready(q)
+            if k < 3:
+                pl.when(jnp.logical_and(interior, in_column))(
+                    lambda: act(pass_copy(k, q, 0, chip(x, y, away[k], core)))
+                )
+            pl.when(in_column)(lambda: act(pass_copy(k, q, 1, chip(x, 1 - y, z, core))))
+            pl.when(over)(lambda: act(pass_copy(k, q, 2, chip(1 - x, y, z, core))))
 
     def hand_on(k):
-        for p in range(2):
-            arrived(order[k], p, x)
-            for condition, copy in passes(k, p):
-                if condition is None:
-                    copy.start()
-                else:
-                    pl.when(condition)(copy.start)
-
-    one = correlator(side, count, None, white, z_parts, y_parts, row_ref, col_ref, stats)
-
+        passes(k, start, lambda q: arrived(order[k], x, q))
+
+    one = correlator(side, count, None, white, z_parts, y_parts, row_table, col_table, stats)
+
+    for copy in loads:
+        copy.wait()
     spectrum_copy.wait_recv()
     for p in range(2):
-        mine = pl.ds(pl.multiple_of(core * half, half), half)
-        theirs = pl.ds(pl.multiple_of((1 - core) * half, half), half)
-        white[p, mine] = spectra_ref[0, p] * weight_ref[mine]
-        white[p, theirs] = spectrum[p] * weight_ref[theirs]
+        for h in range(2):
+            rows = slice(h * half, (h + 1) * half)
+            white[p, rows] = spectrum[h, p] * weight[rows]
 
     hand_on(0)
-    for p in range(2):
-        for h in range(2):
-            arrived(z, p, h)
+    hand_on(1)
+    hand_on(2)
+    for h in range(2):
+        for q in pieces:
+            arrived(z, h, q)
     one(slots.at[z], True)
-    hand_on(1)
     for k in range(3):
-        for p in range(2):
-            arrived(order[k], p, 1 - x)
+        for q in pieces:
+            arrived(order[k], 1 - x, q)
         one(slots.at[order[k]], False)
-        if k == 0:
-            hand_on(2)
 
     stats_copy = [
         pltpu.make_async_remote_copy(
@@ -241,72 +253,60 @@
     for copy in stats_copy:
         copy.start()
     stats_copy[0].wait_recv()
-    peak_ref[0] = jnp.maximum(stats[0, core], other_stats[0])
+    out_ref[0] = jnp.maximum(stats[0, core], other_stats[0])
     stats_copy[1].wait_recv()
-    mean_ref[0] = (stats[1, core] + other_stats[1]) / count
+    out_ref[1] = (stats[1, core] + other_stats[1]) / count
     stats_copy[2].wait_recv()
-    square_ref[0] = (stats[2, core] + other_stats[2]) / count
+    out_ref[2] = (stats[2, core] + other_stats[2]) / count
 
     for copy in stats_copy:
         copy.wait_send()
     spectrum_copy.wait_send()
-    for p in range(2):
-
-        @pl.when(z < 3)
-        def _():
-            first_copy(p, 0, up).wait_send()
-
-        @pl.when(z > 0)
-        def _():
-            first_copy(p, 1, down).wait_send()
-
-        first_copy(p, 2, across).wait_send()
-
-        @pl.when(home != core)
-        def _():
-            first_copy(p, 3, sibling).wait_send()
-
-        for k in range(3):
-            for condition, copy in passes(k, p):
-                if condition is None:
-                    copy.wait_send()
-                else:
-                    pl.when(condition)(copy.wait_send)
+    along(sent)
+    for q in pieces:
+        first_copy(q, 2, across).wait_send()
+        pl.when(home != core)(first_copy(q, 3, sibling).wait_send)
+    for k in range(3):
+        passes(k, sent, lambda q: None)
 
 
 def on_box(spectra, templates, weights):
     side, half = spectra.shape[3], spectra.shape[2]
     count = lax.axis_size("orient") * templates.shape[0]
     rows, cols = tables(side)
-    out = jax.ShapeDtypeStruct((1, half, side), F32)
 
     def body(*refs):
         kernel(side, count, *refs)
 
     vmem = pl.BlockSpec(memory_space=pltpu.VMEM)
-    return pl.pallas_call(
+    maps = pl.pallas_call(
         body,
-        out_shape=(out, out, out),
-        in_specs=[vmem] * 5,
-        out_specs=(vmem, vmem, vmem),
+        out_shape=jax.ShapeDtypeStruct((3, half, side), F32),
+        in_specs=[pl.BlockSpec(memory_space=pl.ANY)] * 5,
+        out_specs=vmem,
         scratch_shapes=[
-            pltpu.VMEM((4, 2, 2, half, side), F32),
-            pltpu.VMEM((2, half, side), F32),
+            pltpu.VMEM((4, 2, 2, 2, half // 2, side), F32),
+            pltpu.VMEM((2, 2, half, side), F32),
+            pltpu.VMEM((side, side), F32),
+            pltpu.VMEM((2, 2 * side, 2 * side), BF16),
+            pltpu.VMEM((2, 2 * side, side), BF16),
             pltpu.VMEM((2, side, side), F32),
             pltpu.VMEM((2, 2 * side, side), BF16),
             pltpu.VMEM((2, side, 2 * side), BF16),
             pltpu.VMEM((3, 2, half, side), F32),
             pltpu.VMEM((3, half, side), F32),
-            pltpu.SemaphoreType.DMA((4, 2)),
-            pltpu.SemaphoreType.DMA((3, 2, 3)),
-            pltpu.SemaphoreType.DMA((4, 2, 2)),
+            pltpu.SemaphoreType.DMA((5, 4)),
+            pltpu.SemaphoreType.DMA((3, 4, 3)),
+            pltpu.SemaphoreType.DMA((4, 2, 4)),
             pltpu.SemaphoreType.DMA((2,)),
             pltpu.SemaphoreType.DMA((2, 3)),
+            pltpu.SemaphoreType.DMA((4,)),
         ],
         compiler_params=pltpu.CompilerParams(
-            collective_id=0, has_side_effects=True, vmem_limit_bytes=48 * 1024 * 1024
+            collective_id=0, has_side_effects=True, vmem_limit_bytes=60 * 1024 * 1024
         ),
     )(spectra, templates, weights, jnp.asarray(rows), jnp.asarray(cols))
+    return (maps[0:1], maps[1:2], maps[2:3])
 
 
 def twiddle(rows, cols, side):

time: 44.1 us -> 36.3 us (0.82)
  local copies, waits for them, and re-layouts: 7.08 us -> 1.78 us
  Pallas kernels: 36.1 us -> 33.8 us
    unnamed x13 -> x0, local copies, waits for them, and re-layouts: 7.08 us -> none
    pallas_call x1, Pallas kernels: 36.1 us -> 33.8 us  [on_box(): pl.pallas_call(body, out_shape=jax.ShapeDtypeStruct((3, half, side), F32)...]
    slice x0 -> x1, local copies, waits for them, and re-layouts: none -> 1.78 us  [on_box(): return (maps[0:1], maps[1:2], maps[2:3])]
where the time goes in v2:
time: 36.3 us; the launch traced here: 36.2 us
  Pallas kernels  33.8 us (93%)
  local copies, waits for them, and re-layouts  1.78 us (5%)
  between operations  0.64 us (2%)
    pallas_call x1, Pallas kernels, on_box(): pl.pallas_call(body, out_shape=jax.ShapeDtypeStruct((3, half, side), F32)...  33.8 us
    slice x1, local copies, waits for them, and re-layouts, on_box(): return (maps[0:1], maps[1:2], maps[2:3])  1.78 us

profile of v2, /device:TPU:0, one launch (start us, length us, event | category | flops | bytes accessed | tf_op | source)
XLA Modules:
  0.0 36.2 jit_solution(11728616461694034033)
XLA Ops:
  0.6 33.8 %shard_map.76 = f32[3,128,256]{2,1,0:T(8,128)} custom-call(f32[1,2,128,256]{3,2,1,0:T(8,128)} %refs_0_.1, f32[1,2,128,256]{3,2,1,0:T(8,128)} %refs_1_.1, f32[256,256]{1,0:T(8,128)} %refs_2_.1, bf16[2,512,512]{2,1,0:T(8,128)(2,1)} %constant.4.clone.refs_3_, bf16[2,512,256]{2,1,0:T(8,128)(2,1)} %constant.5.clone.refs_4_), custom_call_target="tpu_custom_call" | custom-call | tf_op jit(solution)/shard_map/pallas_call | solution.py:282
  34.4 1.8 %fusion = (f32[1,128,256]{2,1,0:T(8,128)}, f32[1,128,256]{2,1,0:T(8,128)}, f32[1,128,256]{2,1,0:T(8,128)}) fusion(f32[3,128,256]{2,1,0:T(8,128)} %shard_map.76), kind=kLoop, calls=%fused_computation | loop fusion | bytes 786432 | tf_op jit(solution)/shard_map/slice | solution.py:309

commit v3 on v2

--- a/solution.py
+++ b/solution.py
@@ -148,7 +148,7 @@
             piece_sem.at[z, core, q],
         )
 
-    up, down, far = chip(x, y, z + 1, home), chip(x, y, z - 1, home), chip(x, y, 3 - z, home)
+    up, down = chip(x, y, z + 1, home), chip(x, y, z - 1, home)
     across, sibling = chip(x, 1 - y, z, home), chip(x, y, z, home)
     chain = x == core
 
@@ -159,7 +159,6 @@
     def along(act):
         for q in pieces:
             near(q, act)
-
 
     def start(copy):
         copy.start()
@@ -176,14 +175,12 @@
         device_id_type=MESH,
     )
     for q in pieces:
-        near(q, start)
+        pl.when(chain)(lambda: near(q, start))
         first_copy(q, 2, across).start()
     spectrum_copy.start()
     for q in pieces:
         pl.when(home != core)(first_copy(q, 3, sibling).start)
         pl.when(home == core)(stay(q).start)
-
-
     def arrived(s, h, q):
         ref = slots.at[s, q // 2, h, q % 2]
         pltpu.make_async_remote_copy(
@@ -191,8 +188,14 @@
             device_id=sibling, device_id_type=MESH,
         ).wait_recv()
 
-    order = (z + 1 - 2 * (z % 2), 2 - z // 2, 3 - 3 * (z // 2))
-    away = (3 - z, 3 * (z // 2), 3 * (z // 2))
+    own = 1 - (z + core + y) % 2
+    beside, across_z = z + 1 - 2 * (z % 2), (z + 2) % 4
+    order = (
+        own * across_z + (1 - own) * beside,
+        own * beside + (1 - own) * (3 - z),
+        own * (3 - z) + (1 - own) * across_z,
+    )
+    away = (own * 3 * (z // 2) + (1 - own) * (3 - z), 3 * (z // 2))
 
     def pass_copy(k, q, way, where):
         ref = slots.at[order[k], q // 2, x, q % 2]
@@ -202,16 +205,15 @@
         )
 
     def passes(k, act, ready):
-        in_column = (core + order[k]) % 2 == y
-        outside = jnp.logical_not(in_column)
-        over = (outside, jnp.logical_or(outside, jnp.logical_not(interior)), z >= 0)[k]
+        in_column = (z >= 0, own == 0, None)[k]
+        over = z >= 0
         for q in pieces:
             ready(q)
-            if k < 3:
+            if k < 2:
                 pl.when(jnp.logical_and(interior, in_column))(
                     lambda: act(pass_copy(k, q, 0, chip(x, y, away[k], core)))
                 )
-            pl.when(in_column)(lambda: act(pass_copy(k, q, 1, chip(x, 1 - y, z, core))))
+                pl.when(in_column)(lambda: act(pass_copy(k, q, 1, chip(x, 1 - y, z, core))))
             pl.when(over)(lambda: act(pass_copy(k, q, 2, chip(1 - x, y, z, core))))
 
     def hand_on(k):
@@ -262,7 +264,7 @@
     for copy in stats_copy:
         copy.wait_send()
     spectrum_copy.wait_send()
-    along(sent)
+    pl.when(chain)(lambda: along(sent))
     for q in pieces:
         first_copy(q, 2, across).wait_send()
         pl.when(home != core)(first_copy(q, 3, sibling).wait_send)

time: 36.3 us -> 35.1 us (0.967)
  Pallas kernels: 33.8 us -> 32.5 us
    pallas_call x1, Pallas kernels: 33.8 us -> 32.5 us  [on_box(): pl.pallas_call(body, out_shape=jax.ShapeDtypeStruct((3, half, side), F32)...]
where the time goes in v3:
time: 35.1 us; the launch traced here: 34.9 us
  Pallas kernels  32.5 us (93%)
  local copies, waits for them, and re-layouts  1.78 us (5%)
  between operations  0.64 us (2%)
    pallas_call x1, Pallas kernels, on_box(): pl.pallas_call(body, out_shape=jax.ShapeDtypeStruct((3, half, side), F32)...  32.5 us
    slice x1, local copies, waits for them, and re-layouts, on_box(): return (maps[0:1], maps[1:2], maps[2:3])  1.78 us

profile of v3, /device:TPU:0, one launch (start us, length us, event | category | flops | bytes accessed | tf_op | source)
XLA Modules:
  0.0 34.9 jit_solution(3681205027480187708)
XLA Ops:
  0.6 32.5 %shard_map.76 = f32[3,128,256]{2,1,0:T(8,128)} custom-call(f32[1,2,128,256]{3,2,1,0:T(8,128)} %refs_0_.1, f32[1,2,128,256]{3,2,1,0:T(8,128)} %refs_1_.1, f32[256,256]{1,0:T(8,128)} %refs_2_.1, bf16[2,512,512]{2,1,0:T(8,128)(2,1)} %constant.4.clone.refs_3_, bf16[2,512,256]{2,1,0:T(8,128)(2,1)} %constant.5.clone.refs_4_), custom_call_target="tpu_custom_call" | custom-call | tf_op jit(solution)/shard_map/pallas_call | solution.py:284
  33.2 1.8 %fusion = (f32[1,128,256]{2,1,0:T(8,128)}, f32[1,128,256]{2,1,0:T(8,128)}, f32[1,128,256]{2,1,0:T(8,128)}) fusion(f32[3,128,256]{2,1,0:T(8,128)} %shard_map.76), kind=kLoop, calls=%fused_computation | loop fusion | bytes 786432 | tf_op jit(solution)/shard_map/slice | solution.py:311
